TPU v7x, 32 devices: a whole 2x2x4 slice. The times are simulated.
32 devices in a mesh: seq: 4 (over y, x), grp: 2 (over core), wsh: 4 (over z).
Axes of the slice: x: 2, y: 2, z: 4, core: 2. Of those that a mesh axis runs over, the one named last changes fastest.
Arguments:
- hidden: bfloat16 [8, 1024, 1536], P(('grp', 'wsh'), 'seq'), may hold values from -6 to 6
- norm_gain: bfloat16 [1536], P('wsh'), may hold values from 0.5 to 1.5
- in_weight: bfloat16 [1536, 6448], P('wsh'), may hold values from -0.15625 to 0.15625
- conv_weight: bfloat16 [3328, 4], P('wsh'), may hold values from -3 to 3
- conv_bias: bfloat16 [3328], P('wsh'), may hold values from -3 to 3
- dt_bias: bfloat16 [48], P('wsh'), may hold values from -13 to -3
- a_log: bfloat16 [48], P('wsh'), may hold values from 0 to 2.7
- skip_gain: bfloat16 [48], P('wsh'), may hold values from 0.5 to 2
- gate_gain: bfloat16 [3072], P('wsh'), may hold values from 0.5 to 1.5
- out_weight: bfloat16 [3072, 1536], P('wsh'), may hold values from -0.109375 to 0.109375
- d_out: bfloat16 [8, 1024, 1536], P(('grp', 'wsh'), 'seq'), may hold values from -6 to 6
Outputs:
- layer_out: bfloat16 [8, 1024, 1536], P(('grp', 'wsh'), 'seq')
- d_hidden: bfloat16 [8, 1024, 1536], P(('grp', 'wsh'), 'seq')
- grad_norm_gain: float32 [1536], P('wsh')
- grad_in_weight: float32 [1536, 6448], P('wsh')
- grad_conv_weight: float32 [3328, 4], P('wsh')
- grad_conv_bias: float32 [3328], P('wsh')
- grad_dt_bias: float32 [48], P('wsh')
- grad_a_log: float32 [48], P('wsh')
- grad_skip_gain: float32 [48], P('wsh')
- grad_gate_gain: float32 [3072], P('wsh')
- grad_out_weight: float32 [3072, 1536], P('wsh')
All inputs are finite; a program needn't handle non-finite values.
Results may differ from a plain program's by a relative error of at most 0.0091.
Values may be sent and summed in bfloat16 or wider, within the bound.
No kernel may reach another device: no remote copies, remote signals or barrier semaphores. Data moves between devices by JAX's collectives and lax.ppermute only.
A program may use at most 320 MiB of HBM per device.

v0:
```python
import jax
import jax.numpy as jnp
from jax import lax
from jax.sharding import PartitionSpec as P

DI = 3072
KCONV = 4
QCH = 256
CONVC = 3328
epsilon = 1e-05
highest = lax.Precision.HIGHEST


def shifted(block, axis, distance):
    devices = range(lax.axis_size(axis))
    route = [(i - distance, i) for i in devices if i - distance in devices]
    return lax.ppermute(block, axis, route)


def rms_apply(values, gain_vec):
    inverse = lax.rsqrt(jnp.mean(values * values, axis=-1, keepdims=True) + epsilon)
    return values * inverse * gain_vec[None, :]


def gated_apply(mixer_out, gate_in, gain_vec):
    product = mixer_out * jax.nn.silu(gate_in)
    inverse = lax.rsqrt(jnp.mean(product * product, axis=-1, keepdims=True) + epsilon)
    return product * inverse * gain_vec[None, :]


def conv_apply(padded, weight, bias_vec):
    tap_count = weight.shape[1]
    row_count = padded.shape[0] - tap_count + 1
    summed = jnp.zeros((row_count, padded.shape[1]), jnp.float32) + bias_vec[None, :]
    for offset in range(tap_count):
        summed = summed + padded[offset : offset + row_count] * weight[:, offset][None, :]
    return jax.nn.silu(summed)


def ssd_apply(x_values, dt_raw, b_and_c, dt_bias, a_log, skip_gain):
    length, head_count = dt_raw.shape
    head_size = x_values.shape[1] // head_count
    state_count = b_and_c.shape[1] // 2
    block_count = length // QCH
    dt_value = jax.nn.softplus(dt_raw + dt_bias[None, :])
    log_rate = -jnp.exp(a_log)[None, :] * dt_value
    causal = (jnp.arange(QCH)[:, None] >= jnp.arange(QCH)[None, :]).astype(jnp.float32)
    x_blocks = x_values.reshape(block_count, QCH, head_count, head_size)
    dt_blocks = dt_value.reshape(block_count, QCH, head_count)
    rate_blocks = log_rate.reshape(block_count, QCH, head_count)
    b_blocks = b_and_c[:, :state_count].reshape(block_count, QCH, state_count)
    c_blocks = b_and_c[:, state_count:].reshape(block_count, QCH, state_count)

    def advance(carried, pieces):
        x_block, dt_block, rate_block, b_block, c_block = pieces
        cumulated = jnp.cumsum(rate_block, axis=0)
        gram_matrix = jnp.dot(c_block, b_block.T, precision=highest)
        spread = cumulated.T[:, :, None] - cumulated.T[:, None, :]
        mixing = (
            jnp.exp(spread * causal[None])
            * causal[None]
            * gram_matrix[None]
            * dt_block.T[:, None, :]
        )
        result = jnp.einsum("hts,shp->thp", mixing, x_block, precision=highest)
        result = (
            result
            + jnp.einsum("tn,hnp->thp", c_block, carried, precision=highest)
            * jnp.exp(cumulated)[:, :, None]
        )
        final_sum = cumulated[-1]
        tail_weight = jnp.exp(final_sum[None, :] - cumulated) * dt_block
        carried = carried * jnp.exp(final_sum)[:, None, None] + jnp.einsum(
            "sn,sh,shp->hnp", b_block, tail_weight, x_block, precision=highest
        )
        return (carried, result)

    initial = jnp.zeros((head_count, state_count, head_size), jnp.float32)
    _, outputs = lax.scan(advance, initial, (x_blocks, dt_blocks, rate_blocks, b_blocks, c_blocks))
    return (
        outputs.reshape(length, head_count * head_size)
        + x_values * jnp.repeat(skip_gain, head_size)[None, :]
    )


def reduce_grads(grads):
    shares = (
        lax.psum_scatter(grads[0], "wsh", scatter_dimension=0, tiled=True),
        lax.psum_scatter(grads[1], "wsh", scatter_dimension=0, tiled=True),
        lax.psum_scatter(grads[2], "wsh", scatter_dimension=0, tiled=True),
        lax.psum_scatter(grads[3], "wsh", scatter_dimension=0, tiled=True),
        lax.psum_scatter(grads[4], "wsh", scatter_dimension=0, tiled=True),
        lax.psum_scatter(grads[5], "wsh", scatter_dimension=0, tiled=True),
        lax.psum_scatter(grads[6], "wsh", scatter_dimension=0, tiled=True),
        lax.psum_scatter(grads[7], "wsh", scatter_dimension=0, tiled=True),
        lax.psum_scatter(grads[8], "wsh", scatter_dimension=0, tiled=True),
    )
    return lax.psum(
        (
            shares[0],
            shares[1],
            shares[2],
            shares[3],
            shares[4],
            shares[5],
            shares[6],
            shares[7],
            shares[8],
        ),
        ("seq", "grp"),
    )


def body(
    hidden,
    norm_gain,
    in_weight,
    conv_weight,
    conv_bias,
    dt_bias,
    a_log,
    skip_gain,
    gate_gain,
    out_weight,
    d_out,
):
    gathered = (
        lax.all_gather(norm_gain, "wsh", axis=0, tiled=True),
        lax.all_gather(in_weight, "wsh", axis=0, tiled=True),
        lax.all_gather(conv_weight, "wsh", axis=0, tiled=True),
        lax.all_gather(conv_bias, "wsh", axis=0, tiled=True),
        lax.all_gather(dt_bias, "wsh", axis=0, tiled=True),
        lax.all_gather(a_log, "wsh", axis=0, tiled=True),
        lax.all_gather(skip_gain, "wsh", axis=0, tiled=True),
    )
    full_norm, full_in, full_conv, full_cbias, full_dtb, full_alog, full_skip = gathered
    tokens_f = hidden[0].astype(jnp.float32)
    cotangent = d_out[0]
    normed_f, rms_back = jax.vjp(rms_apply, tokens_f, full_norm.astype(jnp.float32))
    normed = lax.optimization_barrier(normed_f.astype(jnp.bfloat16))
    projected = lax.optimization_barrier(
        jnp.dot(normed, full_in, preferred_element_type=jnp.float32).astype(jnp.bfloat16)
    )
    gate_part = projected[:, :DI]
    conv_input = projected[:, DI : DI + CONVC]
    dt_part = projected[:, DI + CONVC :]
    rim_rows = shifted(conv_input[conv_input.shape[0] - (KCONV - 1) :], "seq", 1)
    padded = jnp.concatenate([rim_rows, conv_input], axis=0).astype(jnp.float32)
    conved_f, conv_back = jax.vjp(
        conv_apply, padded, full_conv.astype(jnp.float32), full_cbias.astype(jnp.float32)
    )
    conved = lax.optimization_barrier(conved_f.astype(jnp.bfloat16))
    x_heads, dt_heads = (
        lax.all_to_all(conved[:, :DI], "seq", split_axis=1, concat_axis=0, tiled=True),
        lax.all_to_all(dt_part, "seq", split_axis=1, concat_axis=0, tiled=True),
    )
    bc_whole = lax.all_gather(conved[:, DI:], "seq", axis=0, tiled=True)
    local_heads = dt_heads.shape[1]
    head_start = lax.axis_index("seq") * local_heads
    bias_local = lax.dynamic_slice_in_dim(full_dtb.astype(jnp.float32), head_start, local_heads)
    alog_local = lax.dynamic_slice_in_dim(full_alog.astype(jnp.float32), head_start, local_heads)
    skip_local = lax.dynamic_slice_in_dim(full_skip.astype(jnp.float32), head_start, local_heads)
    x_float = x_heads.astype(jnp.float32)
    dt_float = dt_heads.astype(jnp.float32)
    bc_float = bc_whole.astype(jnp.float32)
    y_heads = ssd_apply(x_float, dt_float, bc_float, bias_local, alog_local, skip_local).astype(
        jnp.bfloat16
    )
    y_tokens = lax.all_to_all(y_heads, "seq", split_axis=0, concat_axis=1, tiled=True)
    full_gate, full_out = (
        lax.all_gather(gate_gain, "wsh", axis=0, tiled=True),
        lax.all_gather(out_weight, "wsh", axis=0, tiled=True),
    )
    gated_f, gate_back = jax.vjp(
        gated_apply,
        y_tokens.astype(jnp.float32),
        gate_part.astype(jnp.float32),
        full_gate.astype(jnp.float32),
    )
    gated = gated_f.astype(jnp.bfloat16)
    layer_out = (tokens_f + jnp.dot(gated, full_out, preferred_element_type=jnp.float32)).astype(
        jnp.bfloat16
    )
    grad_out = jnp.einsum("td,te->de", gated, cotangent, preferred_element_type=jnp.float32)
    d_gated = lax.dot_general(
        cotangent, full_out, (((1,), (1,)), ((), ())), preferred_element_type=jnp.float32
    )
    d_mixer, d_gate_part, grad_gate = gate_back(d_gated)
    d_y_heads = lax.all_to_all(
        d_mixer.astype(jnp.bfloat16), "seq", split_axis=1, concat_axis=0, tiled=True
    )
    _, ssd_back = jax.vjp(
        ssd_apply, x_float, dt_float, bc_float, bias_local, alog_local, skip_local
    )
    d_x, d_dt, d_bc_part, grad_dtb, grad_alog, grad_skip = ssd_back(d_y_heads.astype(jnp.float32))
    d_bc = lax.psum_scatter(d_bc_part, "seq", scatter_dimension=0, tiled=True)
    d_x_tokens, d_dt_tokens = (
        lax.all_to_all(d_x.astype(jnp.bfloat16), "seq", split_axis=0, concat_axis=1, tiled=True),
        lax.all_to_all(d_dt.astype(jnp.bfloat16), "seq", split_axis=0, concat_axis=1, tiled=True),
    )
    d_conved = jnp.concatenate([d_x_tokens.astype(jnp.float32), d_bc], axis=1)
    d_padded, grad_conv, grad_cbias = conv_back(d_conved)
    rim_grad = shifted(d_padded[: KCONV - 1].astype(jnp.bfloat16), "seq", -1).astype(jnp.float32)
    own_rows = conv_input.shape[0]
    d_conv_input = d_padded[KCONV - 1 :] + jnp.concatenate(
        [jnp.zeros((own_rows - (KCONV - 1), CONVC), jnp.float32), rim_grad], axis=0
    )
    d_projected = jnp.concatenate(
        [d_gate_part, d_conv_input, d_dt_tokens.astype(jnp.float32)], axis=1
    ).astype(jnp.bfloat16)
    grad_in = jnp.einsum("td,tp->dp", normed, d_projected, preferred_element_type=jnp.float32)
    d_normed = lax.dot_general(
        d_projected, full_in, (((1,), (1,)), ((), ())), preferred_element_type=jnp.float32
    )
    d_tokens, grad_norm = rms_back(d_normed)
    d_hidden = (cotangent.astype(jnp.float32) + d_tokens).astype(jnp.bfloat16)
    all_heads = full_dtb.shape[0]
    placed_dtb = lax.dynamic_update_slice_in_dim(
        jnp.zeros((all_heads,), jnp.float32), grad_dtb, head_start, 0
    )
    placed_alog = lax.dynamic_update_slice_in_dim(
        jnp.zeros((all_heads,), jnp.float32), grad_alog, head_start, 0
    )
    placed_skip = lax.dynamic_update_slice_in_dim(
        jnp.zeros((all_heads,), jnp.float32), grad_skip, head_start, 0
    )
    reduced = reduce_grads(
        (
            grad_norm,
            grad_in,
            grad_conv,
            grad_cbias,
            placed_dtb,
            placed_alog,
            placed_skip,
            grad_gate,
            grad_out,
        )
    )
    return (
        layer_out[None],
        d_hidden[None],
        reduced[0],
        reduced[1],
        reduced[2],
        reduced[3],
        reduced[4],
        reduced[5],
        reduced[6],
        reduced[7],
        reduced[8],
    )


def solution(mesh):
    placed = (
        P(("grp", "wsh"), "seq", None),
        P("wsh"),
        P("wsh", None),
        P("wsh", None),
        P("wsh"),
        P("wsh"),
        P("wsh"),
        P("wsh"),
        P("wsh"),
        P("wsh", None),
        P(("grp", "wsh"), "seq", None),
    )
    return jax.shard_map(
        body,
        mesh=mesh,
        in_specs=placed,
        out_specs=(
            P(("grp", "wsh"), "seq", None),
            P(("grp", "wsh"), "seq", None),
            P("wsh"),
            P("wsh", None),
            P("wsh", None),
            P("wsh"),
            P("wsh"),
            P("wsh"),
            P("wsh"),
            P("wsh"),
            P("wsh", None),
        ),
        check_vma=False,
    )
```

profile of v0, /device:TPU:0, one launch (start us, length us, event | category | flops | bytes accessed | tf_op | source)
XLA Modules:
  0.0 2245.3 jit_solution(12582450332125656297)
XLA Ops:
  9.0 13.6 all-gather
  22.7 13.5 all-gather.1
  37.5 312.8 %all-gather.6.cloned.1.call-done = bf16[1536,6448]{0,1:T(8,128)(2,1)} async-done(((bf16[384,6448]{0,1:T(8,128)(2,1)}), bf16[1536,6448]{0,1:T(8,128)(2,1)}) %all-gather.6.cloned.1.call-update) | async-done | bytes 19808272 | tf_op jit(solution)/shard_map/all_gather | solution.py:129
  350.3 10.3 convolution_convert_fusion
  370.2 10.7 all-reduce.25
  404.4 26.2 %all_gather.36 = bf16[1024,256]{0,1:T(8,128)(2,1)S(1)} all-gather(bf16[256,256]{0,1:T(8,128)(2,1)S(1)} %slice.146), channel_id=1, replica_groups=mesh['seq'=4,'grp'=2,'wsh'=4] {'seq'}, dimensions={0}, use_global_device_ids=true | all-gather | bytes 655360 | tf_op jit(solution)/shard_map/all_gather | solution.py:157
  436.7 52.1 %while.86 = (s32[]{:T(128)}, f32[12,128,64]{1,2,0:T(8,128)}, f32[4,256,12,64]{1,3,2,0:T(8,128)}, f32[4,256,12]{1,2,0:T(8,128)}, f32[4,256,12]{1,2,0:T(8,128)S(1)...) while((s32[]{:T(128)}, f32[12,128,64]{1,2,0:T(8,128)}, ...), condition=%wide.region_4.5_spmd.clone.clone, body=%wide.region_1.4_spmd.clone.clone.sunk | while | flops 1313970176 | bytes 8233615 | solution.py:79
  497.3 19.0 all-gather.2
  545.9 128.5 %while.87 = (s32[]{:T(128)}, f32[12,128,64]{1,2,0:T(8,128)}, f32[4,128,256]{1,2,0:T(8,128)}, f32[4,12,256,256]{3,2,1,0:T(8,128)}, f32[4,1,256,256]{3,2,1,0:T(8,1...) while((s32[]{:T(128)}, f32[12,128,64]{1,2,0:T(8,128)}, ...), condition=%wide.region_10.11_spmd.clone.clone, body=%wide.region_7.10_spmd.clone.clone.sunk | while | flops 709793792 | bytes 22214624 | solution.py:79
  682.6 290.8 %while.88 = (s32[]{:T(128)}, f32[12,128,64]{1,2,0:T(8,128)S(1)}, f32[4,256,12,64]{1,3,2,0:T(8,128)}, f32[4,256,12]{1,2,0:T(8,128)}, f32[4,256,12]{1,2,0:T(8,128)...) while((s32[]{:T(128)}, f32[12,128,64]{1,2,0:T(8,128)S(1)}, ...), condition=%wide.region_21.22_spmd.clone.clone, body=%wide.region_11.21_spmd.clone.clone.sunk | while | flops 2628807680 | bytes 29113356 | solution.py:79
  781.1 9.3 fusion.282
  853.7 9.3 fusion.282
  926.3 9.4 fusion.282
  980.1 9.4 fusion.176
  992.9 24.3 %all_to_all.69 = bf16[4,256,768]{1,2,0:T(8,128)(2,1)S(1)} all-to-all(bf16[4,256,768]{1,2,0:T(8,128)(2,1)S(1)} %fusion.161), channel_id=1, replica_groups=mesh['seq'=4,'grp'=2,'wsh'=4] {'seq'}, dimensions={0} | all-to-all | bytes 3145728 | tf_op jit(solution)/shard_map/all_to_all | solution.py:198
  1019.2 12.2 multiply_reduce_fusion.3
  1044.5 9.7 all_to_all.70
  1060.5 19.0 fusion.173
  1081.5 252.9 %reduce-scatter.11.cloned.1.call-done = f32[768,1536]{1,0:T(8,128)} async-done(((f32[3072,1536]{1,0:T(8,128)}), f32[768,1536]{1,0:T(8,128)}) %reduce-scatter.11.cloned.1.call-update) | async-done | bytes 4718608 | tf_op jit(solution)/shard_map/reduce_scatter | solution.py:96
  1334.4 651.6 %reduce-scatter.9.cloned.1.call-done = f32[384,6448]{0,1:T(8,128)} async-done(((f32[1536,6448]{0,1:T(8,128)}), f32[384,6448]{0,1:T(8,128)}) %reduce-scatter.9.cloned.1.call-update) | async-done | bytes 9904144 | tf_op jit(solution)/shard_map/reduce_scatter | solution.py:89
  1999.9 14.0 fusion.168
  2013.9 21.4 all-reduce.24
  2039.8 24.8 %all-reduce.22 = (f32[384]{0:T(512)}, f32[832,4]{0,1:T(4,128)}, f32[832]{0:T(1024)}, f32[12]{0:T(128)}, f32[12]{0:T(128)}, /*index=5*/f32[12]{0:T(128)}, f32[768]{0:T(1024)}) all-reduce(f32[384]{0:T(512)S(1)} %dynamic-slice.5, f32[832,4]{0,1:T(4,128)S(1)} %copy.193, ...), channel_id=1, replica_groups=mesh['seq'=4,'grp'=2,'wsh'=4] {'seq','grp'}, use_global_device_ids=true, to_apply=%region_26.27 | all-reduce | flops 5348 | bytes 42784 | tf_op jit(solution)/shard_map/psum | solution.py:98
  2064.6 163.0 %all-reduce.28.cloned.1.call-done = (f32[384,6448]{0,1:T(8,128)}, f32[768,1536]{1,0:T(8,128)}) async-done(((f32[384,6448]{0,1:T(8,128)}, f32[768,1536]{1,0:T(8,128)}), (f32[384,6448]{0,1:T(8,128)}, f32[768,1536]{1,0:T(8,128)})) %all-reduce.28.cloned.1.call-update) | async-done | bytes 14622736 | tf_op jit(solution)/shard_map/psum | solution.py:98
  (620 shorter events, 588.6 us)
Async XLA Ops:
  7.2 343.1 %all-gather.6.cloned.1.call-start = ((), (), s32[]{:S(2)}) async-start(), calls=%async_computation.10 | async-start | bytes 24760320 | tf_op jit(solution)/shard_map/all_gather | solution.py:129
  7.9 513.5 %all-gather.8.cloned.1.call-start = ((), (), s32[]{:S(2)}) async-start(), calls=%async_computation.11 | async-start | bytes 11796480 | tf_op jit(solution)/shard_map/all_gather | solution.py:172
  9.0 351.7 %copy-start.37 = (f32[256]{0:T(256)}, f32[256]{0:T(256)S(1)}, u32[]{:S(2)}) copy-start(f32[256]{0:T(256)S(1)} %fusion.187) | copy-start | bytes 3076
  22.7 338.0 %copy-start.29 = (f32[1536]{0:T(1024)}, f32[1536]{0:T(1024)S(1)}, u32[]{:S(2)}) copy-start(f32[1536]{0:T(1024)S(1)} %reshape.483) | copy-start | bytes 18436
  37.5 329.9 %copy-start.46 = (u32[32]{0:T(128)S(1)}, u32[32]{0:T(128)}, u32[]{:S(2)}) copy-start(u32[32]{0:T(128)} %constant.226) | copy-start | bytes 388
  37.5 331.8 %copy-start.52 = (bf16[12]{0:T(256)(128)(2,1)S(1)}, bf16[12]{0:T(256)(128)(2,1)}, u32[]{:S(2)}) copy-start(bf16[12]{0:T(256)(128)(2,1)} %param.22) | copy-start | bytes 76
  37.5 332.0 %copy-start.53 = (bf16[12]{0:T(256)(128)(2,1)S(1)}, bf16[12]{0:T(256)(128)(2,1)}, u32[]{:S(2)}) copy-start(bf16[12]{0:T(256)(128)(2,1)} %param.23) | copy-start | bytes 76
  37.5 332.3 %copy-start.54 = (bf16[12]{0:T(256)(128)(2,1)S(1)}, bf16[12]{0:T(256)(128)(2,1)}, u32[]{:S(2)}) copy-start(bf16[12]{0:T(256)(128)(2,1)} %param.24) | copy-start | bytes 76
  37.5 332.5 %copy-start.47 = (bf16[832]{0:T(1024)(128)(2,1)S(1)}, bf16[832]{0:T(1024)(128)(2,1)}, u32[]{:S(2)}) copy-start(bf16[832]{0:T(1024)(128)(2,1)} %param.21) | copy-start | bytes 4996
  360.7 22.3 copy-start.6
  363.9 22.6 %collective-permute-start = (bf16[3,3328]{1,0:T(4,128)(2,1)S(1)}, bf16[3,3328]{1,0:T(4,128)(2,1)S(1)}, u32[]{:S(2)}, u32[]{:S(2)}) collective-permute-start(bf16[3,3328]{1,0:T(4,128)(2,1)S(1)} %copy.162), channel_id=1, source_target_pairs={{0,8},{8,16},{16,24},{1,9},{9,17},{17,25},{2,10},{10,18},{18,26},{... | collective-permute-start | bytes 59912 | tf_op jit(solution)/shard_map/ppermute | solution.py:17
  367.3 22.2 copy-start.21
  382.9 14.8 all-to-all-start
  397.8 35.0 %all-to-all-start.1 = ((bf16[256,4,768]{0,2,1:T(8,128)(2,1)}), bf16[256,4,768]{0,2,1:T(8,128)(2,1)}, u32[]{:S(2)}, u32[]{:S(2)}) async-start(bf16[256,4,768]{0,2,1:T(8,128)(2,1)} %bitcast.6), calls=%async_computation.1 | async-start | bytes 3145728 | tf_op jit(solution)/shard_map/all_to_all | solution.py:154
  492.7 23.6 %all-to-all-start.2 = ((bf16[4,256,768]{1,2,0:T(8,128)(2,1)}), bf16[4,256,768]{1,2,0:T(8,128)(2,1)}, u32[]{:S(2)}, u32[]{:S(2)}) async-start(bf16[4,256,768]{1,2,0:T(8,128)(2,1)} %fusion.162), calls=%async_computation.2 | async-start | bytes 3145728 | tf_op jit(solution)/shard_map/all_to_all | solution.py:169
  535.4 138.9 %all-to-all-start.3 = ((bf16[256,4,768]{0,2,1:T(8,128)(2,1)}), bf16[256,4,768]{0,2,1:T(8,128)(2,1)}, u32[]{:S(2)}, u32[]{:S(2)}) async-start(bf16[256,4,768]{0,2,1:T(8,128)(2,1)} %bitcast.595), calls=%async_computation.3 | async-start | bytes 3145728 | tf_op jit(solution)/shard_map/all_to_all | solution.py:189
  539.7 479.4 %reduce-scatter.7.cloned.1.call-start = ((), (), s32[]{:S(2)}) async-start(), calls=%async_computation.12 | async-start | bytes 1310720 | tf_op jit(solution)/shard_map/reduce_scatter | solution.py:196
  980.0 354.4 %reduce-scatter.11.cloned.1.call-start = ((), (), s32[]{:S(2)}) async-start(), calls=%async_computation.14 | async-start | bytes 23592960 | tf_op jit(solution)/shard_map/reduce_scatter | solution.py:96
  989.5 996.6 %reduce-scatter.9.cloned.1.call-start = ((), (), s32[]{:S(2)}) async-start(), calls=%async_computation.13 | async-start | bytes 49520640 | tf_op jit(solution)/shard_map/reduce_scatter | solution.py:89
  1042.9 11.4 collective-permute-start.1
  1079.5 959.1 %reduce-scatter.13.cloned.1.call-start = ((), (), s32[]{:S(2)}) async-start(), calls=%async_computation.15 | async-start | bytes 2129920
  1081.4 1146.1 %all-reduce.28.cloned.1.call-start = ((), (), s32[]{:S(2)}) async-start(), calls=%async_computation.16 | async-start | bytes 29245440 | tf_op jit(solution)/shard_map/psum | solution.py:98
  1999.9 35.8 %copy-start.36 = (f32[256]{0:T(256)S(1)}, f32[256]{0:T(256)}, u32[]{:S(2)}) copy-start(f32[256]{0:T(256)} %copy-done.35) | copy-start | bytes 3076
  1999.9 35.8 %copy-start.13 = (bf16[1,256,1536]{2,1,0:T(8,128)(2,1)S(1)}, bf16[1,256,1536]{2,1,0:T(8,128)(2,1)}, u32[]{:S(2)}) copy-start(bf16[1,256,1536]{2,1,0:T(8,128)(2,1)} %param.27) | copy-start | bytes 2359300
  (53 other events, 395.0 us)
Sparse Core Ops, SparseCore 0:
  9.6 340.6 all-gather.5
  351.9 166.4 all-gather.7
  980.1 36.9 reduce-scatter.6
  1019.4 315.0 reduce-scatter.10
  1336.6 649.3 reduce-scatter.8
  1988.8 40.4 reduce-scatter.12
  2033.1 194.4 all-reduce.27
where the time goes:
time: 2260 us; the launch traced here: 2250 us
  waiting for transfers between devices  1380 us (61%)
  matrix products  257 us (11%)
  local copies, waits for them, and re-layouts  225 us (10%)
  other arithmetic  176 us (8%)
  blocking collectives  163 us (7%)
    reduce_scatter x1, waiting for transfers between devices, reduce_grads(): lax.psum_scatter(grads[1], 'wsh', scatter_dimension=0, tiled=True)  652 us
    all_gather x1, waiting for transfers between devices, body(): lax.all_gather(in_weight, 'wsh', axis=0, tiled=True)  313 us
    reduce_scatter x1, waiting for transfers between devices, reduce_grads(): lax.psum_scatter(grads[8], 'wsh', scatter_dimension=0, tiled=True)  253 us
    psum x1, waiting for transfers between devices, reduce_grads(): lax.psum((shares[0], shares[1], shares[2], shares[3], shares[4], shares[5...  163 us
    dot_general x12, matrix products, advance(): result = jnp.einsum('hts,shp->thp', mixing, x_block, precision=highest)  77.1 us
    another operation x42, other arithmetic  46.3 us
  transfers between devices with their start and end apart: 13, of which 4 were waited for; matrix products, arithmetic and copies ran while one was open for 14% of the time, Pallas kernels for 0%

commit v1 on v0

--- a/solution.py
+++ b/solution.py
@@ -9,6 +9,27 @@
 CONVC = 3328
 epsilon = 1e-05
 highest = lax.Precision.HIGHEST
+
+
+def gather_around(x, axis, dim):
+    size, index, width = (lax.axis_size(axis), lax.axis_index(axis), x.shape[dim])
+    ahead = [(i, (i + 1) % size) for i in range(size)]
+    behind = [(i, (i - 1) % size) for i in range(size)]
+    whole = jnp.zeros((*x.shape[:dim], size * width, *x.shape[dim + 1 :]), x.dtype)
+    whole = lax.dynamic_update_slice_in_dim(whole, x, index * width, axis=dim)
+    from_left = from_right = x
+    halfway = size // 2
+    for step in range(1, halfway + 1):
+        from_left = lax.ppermute(from_left, axis, ahead)
+        whole = lax.dynamic_update_slice_in_dim(
+            whole, from_left, (index - step) % size * width, axis=dim
+        )
+        if step < size - halfway:
+            from_right = lax.ppermute(from_right, axis, behind)
+            whole = lax.dynamic_update_slice_in_dim(
+                whole, from_right, (index + step) % size * width, axis=dim
+            )
+    return whole
 
 
 def shifted(block, axis, distance):
@@ -126,7 +147,7 @@
 ):
     gathered = (
         lax.all_gather(norm_gain, "wsh", axis=0, tiled=True),
-        lax.all_gather(in_weight, "wsh", axis=0, tiled=True),
+        gather_around(in_weight, "wsh", 0),
         lax.all_gather(conv_weight, "wsh", axis=0, tiled=True),
         lax.all_gather(conv_bias, "wsh", axis=0, tiled=True),
         lax.all_gather(dt_bias, "wsh", axis=0, tiled=True),

time: 2260 us -> 2380 us (1.053)
  blocking collectives: 163 us -> 498 us
  waiting for transfers between devices: 1380 us -> 1170 us
    all_gather x1, blocking collectives: 13.6 us -> 368 us  [body(): lax.all_gather(norm_gain, 'wsh', axis=0, tiled=True)]
    all_gather x1 -> x0, waiting for transfers between devices: 313 us -> none  [body(): lax.all_gather(in_weight, 'wsh', axis=0, tiled=True)]
    ppermute x0 -> x3, waiting for transfers between devices: none -> 108 us  [the longest x2 108 us: gather_around(): from_left = lax.ppermute(from_left, axis, ahead)]
  transfers between devices with their start and end apart: 13 -> 15, of which waited for: 4 -> 4; matrix products, arithmetic and copies ran while one was open for 14% -> 15% of each run, Pallas kernels for 0% -> 0%
where the time goes in v1:
time: 2380 us; the launch traced here: 2360 us
  waiting for transfers between devices  1170 us (49%)
  blocking collectives  498 us (21%)
  matrix products  242 us (10%)
  local copies, waits for them, and re-layouts  216 us (9%)
  other arithmetic  182 us (8%)
  starting transfers between devices  27.2 us (1%)
    reduce_scatter x1, waiting for transfers between devices, reduce_grads(): lax.psum_scatter(grads[1], 'wsh', scatter_dimension=0, tiled=True)  652 us
    all_gather x1, blocking collectives, body(): lax.all_gather(norm_gain, 'wsh', axis=0, tiled=True)  368 us
    reduce_scatter x1, waiting for transfers between devices, reduce_grads(): lax.psum_scatter(grads[8], 'wsh', scatter_dimension=0, tiled=True)  251 us
    psum x1, waiting for transfers between devices, reduce_grads(): lax.psum((shares[0], shares[1], shares[2], shares[3], shares[4], shares[5...  163 us
    ppermute x2, waiting for transfers between devices, gather_around(): from_left = lax.ppermute(from_left, axis, ahead)  108 us
    dot_general x12, matrix products, advance(): result = jnp.einsum('hts,shp->thp', mixing, x_block, precision=highest)  78.4 us
    another operation x73, local copies, waits for them, and re-layouts  56.5 us
    another operation x42, other arithmetic  49 us
  transfers between devices with their start and end apart: 15, of which 4 were waited for; matrix products, arithmetic and copies ran while one was open for 15% of the time, Pallas kernels for 0%

profile of v1, /device:TPU:0, one launch (start us, length us, event | category | flops | bytes accessed | tf_op | source)
XLA Modules:
  0.0 2360.2 jit_solution(4153259348875429102)
XLA Ops:
  12.4 108.0 %collective-permute-done = bf16[384,6448]{0,1:T(8,128)(2,1)} collective-permute-done((bf16[384,6448]{0,1:T(8,128)(2,1)}, bf16[384,6448]{0,1:T(8,128)(2,1)}, u32[]{:S(2)}, u32[]{:S(2)}) %collective-permute-start) | collective-permute-done | bytes 4952096 | tf_op jit(solution)/shard_map/ppermute | solution.py:23
  121.2 367.8 %all-gather = bf16[4,1,384]{2,1,0:T(2,128)(2,1)S(1)} all-gather(bf16[1,1,384]{2,1,0:T(2,128)(2,1)S(1)} %reshape.477), channel_id=1, replica_groups=mesh['seq'=4,'grp'=2,'wsh'=4] {'wsh'}, dimensions={0}, use_global_device_ids=true | all-gather | bytes 3840 | tf_op jit(solution)/shard_map/all_gather | solution.py:149
  492.1 13.2 all-gather.1
  537.0 10.9 all-reduce.25
  571.3 16.7 all_gather.32
  593.8 79.0 %while.86 = (s32[]{:T(128)}, f32[12,128,64]{1,2,0:T(8,128)S(1)}, f32[4,256,12,64]{1,3,2,0:T(8,128)}, f32[4,256,12]{1,2,0:T(8,128)}, f32[4,256,12]{1,2,0:T(8,128)...) while((s32[]{:T(128)}, f32[12,128,64]{1,2,0:T(8,128)S(1)}, ...), condition=%wide.region_4.5_spmd.clone.clone, body=%wide.region_1.4_spmd.clone.clone.sunk | while | flops 1313970176 | bytes 7890463 | solution.py:100
  681.7 13.7 all-gather.2
  725.0 124.5 %while.87 = (s32[]{:T(128)}, f32[12,128,64]{1,2,0:T(8,128)}, f32[4,128,256]{1,2,0:T(8,128)}, f32[4,12,256,256]{3,2,1,0:T(8,128)}, f32[4,1,256,256]{3,2,1,0:T(8,1...) while((s32[]{:T(128)}, f32[12,128,64]{1,2,0:T(8,128)}, ...), condition=%wide.region_10.11_spmd.clone.clone, body=%wide.region_7.10_spmd.clone.clone.sunk | while | flops 709793792 | bytes 22276536 | solution.py:100
  857.7 236.7 %while.88 = (s32[]{:T(128)}, f32[12,128,64]{1,2,0:T(8,128)S(1)}, f32[4,256,12,64]{1,3,2,0:T(8,128)}, f32[4,256,12]{1,2,0:T(8,128)}, f32[4,256,12]{1,2,0:T(8,128)...) while((s32[]{:T(128)}, f32[12,128,64]{1,2,0:T(8,128)S(1)}, ...), condition=%wide.region_21.22_spmd.clone.clone, body=%wide.region_11.21_spmd.clone.clone.sunk | while | flops 2628807680 | bytes 44792864 | solution.py:100
  869.4 9.3 fusion.282
  928.5 9.3 fusion.282
  987.6 9.3 fusion.282
  1046.6 9.3 fusion.282
  1101.1 9.4 fusion.176
  1114.0 20.4 all_to_all.69
  1136.4 12.2 multiply_reduce_fusion.3
  1161.7 9.2 all_to_all.70
  1177.2 19.0 fusion.173
  1198.2 251.2 %reduce-scatter.11.cloned.1.call-done = f32[768,1536]{1,0:T(8,128)} async-done(((f32[3072,1536]{1,0:T(8,128)}), f32[768,1536]{1,0:T(8,128)}) %reduce-scatter.11.cloned.1.call-update) | async-done | bytes 4718608 | tf_op jit(solution)/shard_map/reduce_scatter | solution.py:117
  1449.4 651.6 %reduce-scatter.9.cloned.1.call-done = f32[384,6448]{0,1:T(8,128)} async-done(((f32[1536,6448]{0,1:T(8,128)}), f32[384,6448]{0,1:T(8,128)}) %reduce-scatter.9.cloned.1.call-update) | async-done | bytes 9904144 | tf_op jit(solution)/shard_map/reduce_scatter | solution.py:110
  2114.9 14.0 fusion.168
  2128.9 21.3 all-reduce.24
  2154.6 24.8 %all-reduce.22 = (f32[384]{0:T(512)}, f32[832,4]{0,1:T(4,128)}, f32[832]{0:T(1024)}, f32[12]{0:T(128)}, f32[12]{0:T(128)}, /*index=5*/f32[12]{0:T(128)}, f32[768]{0:T(1024)}) all-reduce(f32[384]{0:T(512)S(1)} %dynamic-slice.5, f32[832,4]{0,1:T(4,128)S(1)} %copy.193, ...), channel_id=1, replica_groups=mesh['seq'=4,'grp'=2,'wsh'=4] {'seq','grp'}, use_global_device_ids=true, to_apply=%region_26.27 | all-reduce | flops 5348 | bytes 42784 | tf_op jit(solution)/shard_map/psum | solution.py:119
  2179.4 163.0 %all-reduce.28.cloned.1.call-done = (f32[384,6448]{0,1:T(8,128)}, f32[768,1536]{1,0:T(8,128)}) async-done(((f32[384,6448]{0,1:T(8,128)}, f32[768,1536]{1,0:T(8,128)}), (f32[384,6448]{0,1:T(8,128)}, f32[768,1536]{1,0:T(8,128)})) %all-reduce.28.cloned.1.call-update) | async-done | bytes 14622736 | tf_op jit(solution)/shard_map/psum | solution.py:119
  (668 shorter events, 576.3 us)
Async XLA Ops:
  7.2 483.8 %copy-start.7 = (bf16[1,256,1536]{2,1,0:T(8,128)(2,1)S(1)}, bf16[1,256,1536]{2,1,0:T(8,128)(2,1)}, u32[]{:S(2)}) copy-start(bf16[1,256,1536]{2,1,0:T(8,128)(2,1)} %param.17) | copy-start | bytes 2359300
  7.2 484.9 %copy-start.47 = (bf16[832,4]{0,1:T(4,128)(2,1)S(1)}, bf16[832,4]{0,1:T(4,128)(2,1)}, u32[]{:S(2)}) copy-start(bf16[832,4]{0,1:T(4,128)(2,1)} %param.20) | copy-start | bytes 19972
  7.2 693.3 %all-gather.5.cloned.1.call-start = ((), (), s32[]{:S(2)}) async-start(), calls=%async_computation.10 | async-start | bytes 11796480 | tf_op jit(solution)/shard_map/all_gather | solution.py:193
  7.2 113.2 %collective-permute-start = (bf16[384,6448]{0,1:T(8,128)(2,1)}, bf16[384,6448]{0,1:T(8,128)(2,1)}, u32[]{:S(2)}, u32[]{:S(2)}) collective-permute-start(bf16[384,6448]{0,1:T(8,128)(2,1)} %param.19), channel_id=1, source_target_pairs={{0,1},{1,2},{2,3},{3,0},{4,5},{5,6},{6,7},{7,4},{8,9},{9,10},{10,1... | collective-permute-start | bytes 14856200 | tf_op jit(solution)/shard_map/ppermute | solution.py:23
  10.3 503.4 %collective-permute-start.1 = (bf16[384,6448]{0,1:T(8,128)(2,1)}, bf16[384,6448]{0,1:T(8,128)(2,1)}, u32[]{:S(2)}, u32[]{:S(2)}) collective-permute-start(bf16[384,6448]{0,1:T(8,128)(2,1)} %param.19), channel_id=1, source_target_pairs={{0,3},{1,0},{2,1},{3,2},{4,7},{5,4},{6,5},{7,6},{8,11},{9,8},{10,9... | collective-permute-start | bytes 14856200 | tf_op jit(solution)/shard_map/ppermute | solution.py:28
  120.4 396.8 %collective-permute-start.2 = (bf16[384,6448]{0,1:T(8,128)(2,1)}, bf16[384,6448]{0,1:T(8,128)(2,1)}, u32[]{:S(2)}, u32[]{:S(2)}) collective-permute-start(bf16[384,6448]{0,1:T(8,128)(2,1)} %collective-permute-done), channel_id=1, source_target_pairs={{0,1},{1,2},{2,3},{3,0},{4,5},{5,6},{6,7},{7,4},{8,9},{9,10},{10,1... | collective-permute-start | bytes 14856200 | tf_op jit(solution)/shard_map/ppermute | solution.py:23
  527.5 22.3 copy-start.9
  530.5 22.9 collective-permute-start.3
  534.0 22.4 copy-start.23
  534.0 22.4 copy-start.25
  534.0 22.4 copy-start.27
  534.1 22.4 copy-start.29
  549.8 14.8 all-to-all-start
  564.6 25.5 %all-to-all-start.1 = ((bf16[256,4,768]{0,2,1:T(8,128)(2,1)}), bf16[256,4,768]{0,2,1:T(8,128)(2,1)}, u32[]{:S(2)}, u32[]{:S(2)}) async-start(bf16[256,4,768]{0,2,1:T(8,128)(2,1)} %bitcast.6), calls=%async_computation.1 | async-start | bytes 3145728 | tf_op jit(solution)/shard_map/all_to_all | solution.py:175
  676.8 18.5 all-to-all-start.2
  714.4 135.0 %all-to-all-start.3 = ((bf16[256,4,768]{0,2,1:T(8,128)(2,1)}), bf16[256,4,768]{0,2,1:T(8,128)(2,1)}, u32[]{:S(2)}, u32[]{:S(2)}) async-start(bf16[256,4,768]{0,2,1:T(8,128)(2,1)} %bitcast.595), calls=%async_computation.3 | async-start | bytes 3145728 | tf_op jit(solution)/shard_map/all_to_all | solution.py:210
  718.8 417.5 %reduce-scatter.7.cloned.1.call-start = ((), (), s32[]{:S(2)}) async-start(), calls=%async_computation.11 | async-start | bytes 1310720 | tf_op jit(solution)/shard_map/reduce_scatter | solution.py:217
  1101.0 348.4 %reduce-scatter.11.cloned.1.call-start = ((), (), s32[]{:S(2)}) async-start(), calls=%async_computation.13 | async-start | bytes 23592960 | tf_op jit(solution)/shard_map/reduce_scatter | solution.py:117
  1110.5 990.6 %reduce-scatter.9.cloned.1.call-start = ((), (), s32[]{:S(2)}) async-start(), calls=%async_computation.12 | async-start | bytes 49520640 | tf_op jit(solution)/shard_map/reduce_scatter | solution.py:110
  1160.1 10.8 collective-permute-start.4
  1196.2 957.2 %reduce-scatter.13.cloned.1.call-start = ((), (), s32[]{:S(2)}) async-start(), calls=%async_computation.14 | async-start | bytes 2129920
  1198.2 1144.3 %all-reduce.28.cloned.1.call-start = ((), (), s32[]{:S(2)}) async-start(), calls=%async_computation.15 | async-start | bytes 29245440 | tf_op jit(solution)/shard_map/psum | solution.py:119
  2114.9 35.8 %copy-start.42 = (f32[256]{0:T(256)S(1)}, f32[256]{0:T(256)}, u32[]{:S(2)}) copy-start(f32[256]{0:T(256)} %copy-done.41) | copy-start | bytes 3076
  2114.9 35.8 %copy-start.15 = (bf16[1,256,1536]{2,1,0:T(8,128)(2,1)S(1)}, bf16[1,256,1536]{2,1,0:T(8,128)(2,1)}, u32[]{:S(2)}) copy-start(bf16[1,256,1536]{2,1,0:T(8,128)(2,1)} %param.27) | copy-start | bytes 2359300
  (75 other events, 549.8 us)
Sparse Core Ops, SparseCore 0:
  120.5 363.3 all-gather.4
  1101.1 33.5 reduce-scatter.6
  1137.1 312.3 reduce-scatter.10
  1451.7 649.3 reduce-scatter.8
  2103.8 40.4 reduce-scatter.12
  2147.9 194.4 all-reduce.27
